TPU v7x, 32 devices: a whole 2x2x4 slice. The times are simulated.
32 devices in a mesh: shard: 4 (over y, x), ctx: 2 (over core), tp: 4 (over z).
Axes of the slice: x: 2, y: 2, z: 4, core: 2. Of those that a mesh axis runs over, the one named last changes fastest.
Arguments:
- tokens: bfloat16 [4, 1024, 1536], P('shard', ('ctx', 'tp')), may hold values from -6 to 6
- cotangent: bfloat16 [4, 1024, 1536], P('shard', ('ctx', 'tp')), may hold values from -6 to 6
- lengths: int32 [4], P('shard'), may hold values from 256 to 1024, as said below
- w_qkv: bfloat16 [1536, 3, 1536], P(('shard', 'ctx'), None, 'tp'), may hold values from -0.15625 to 0.15625
- w_forget: bfloat16 [1536, 24], P(('shard', 'ctx'), 'tp'), may hold values from -0.15625 to 0.15625
- forget_bias: float32 [24], replicated, may hold values from 3 to 8
- w_ogate: bfloat16 [1536, 1536], P(('shard', 'ctx'), 'tp'), may hold values from -0.15625 to 0.15625
- w_out: bfloat16 [1536, 1536], P(('shard', 'ctx'), 'tp'), may hold values from -0.625 to 0.625
- w_gu: bfloat16 [1536, 2, 4096], P(('shard', 'ctx'), None, 'tp'), may hold values from -0.15625 to 0.15625
- w_down: bfloat16 [1536, 4096], P(('shard', 'ctx'), 'tp'), may hold values from -0.09375 to 0.09375
- gain_attn: float32 [1536], replicated, may hold values from 0.5 to 1.5
- gain_mlp: float32 [1536], replicated, may hold values from 0.5 to 1.5
- qk_gain: float32 [2, 64], replicated, may hold values from 1 to 2
Outputs:
- output: bfloat16 [4, 1024, 1536], P('shard', ('ctx', 'tp'))
- input_grad: bfloat16 [4, 1024, 1536], P('shard', ('ctx', 'tp'))
- grad_qkv: float32 [1536, 3, 1536], P(('shard', 'ctx'), None, 'tp')
- grad_forget: float32 [1536, 24], P(('shard', 'ctx'), 'tp')
- grad_forget_bias: float32 [24], replicated
- grad_ogate: float32 [1536, 1536], P(('shard', 'ctx'), 'tp')
- grad_out: float32 [1536, 1536], P(('shard', 'ctx'), 'tp')
- grad_gu: float32 [1536, 2, 4096], P(('shard', 'ctx'), None, 'tp')
- grad_down: float32 [1536, 4096], P(('shard', 'ctx'), 'tp')
- grad_gain_attn: float32 [1536], replicated
- grad_gain_mlp: float32 [1536], replicated
- grad_qk_gain: float32 [2, 64], replicated
Inputs may be any that keep to these rules, and one draw needn't show every extreme that they name: `lengths`: real tokens of a slot; positions at or past it are padding; both the least and the most value occur in every draw.
All inputs are finite; a program needn't handle non-finite values.
Results may differ from a plain program's by a relative error of at most 0.04.
Values may be sent and summed in bfloat16 or wider, within the bound.
No kernel may reach another device: no remote copies, remote signals or barrier semaphores. Data moves between devices by JAX's collectives and lax.ppermute only.
A program may use at most 128 MiB of HBM per device.

v0:
```python
import math
import jax
import jax.numpy as jnp
from jax import lax
from jax.sharding import PartitionSpec as P

epsilon = 1e-06


def shifted(block, axis, distance):
    devices = range(lax.axis_size(axis))
    route = [(i - distance, i) for i in devices if i - distance in devices]
    return lax.ppermute(block, axis, route)


def norm_rows(values, gain):
    return values * lax.rsqrt(jnp.mean(values * values, axis=-1, keepdims=True) + epsilon) * gain


def product(left, right):
    return jnp.dot(left, right, preferred_element_type=jnp.float32)


def product_t(left, right):
    return lax.dot_general(
        left, right, (((1,), (1,)), ((), ())), preferred_element_type=jnp.float32
    )


def outer_rows(left, right):
    return lax.dot_general(
        left, right, (((0,), (0,)), ((), ())), preferred_element_type=jnp.float32
    )


def body(
    tokens,
    cotangent,
    lengths,
    w_qkv,
    w_forget,
    forget_bias,
    w_ogate,
    w_out,
    w_gu,
    w_down,
    gain_attn,
    gain_mlp,
    qk_gain,
):
    slot_count, own_rows, model_width = tokens.shape
    tensor_size = lax.axis_size("tp")
    tensor_place = lax.axis_index("tp")
    span_index = lax.axis_index("ctx")
    half_rows = own_rows * tensor_size
    row_count = slot_count * half_rows
    local_heads = w_forget.shape[1]
    head_size = qk_gain.shape[1]
    head_cols = local_heads * head_size
    hidden_units = w_down.shape[1]
    item_count = slot_count * local_heads
    score_scale = 1.0 / math.sqrt(head_size)
    own_start = tensor_place * own_rows
    full_tokens, full_cot = (
        lax.all_gather(tokens, "tp", axis=1, tiled=True),
        lax.all_gather(cotangent, "tp", axis=1, tiled=True),
    )
    qkv_full, forget_full, ogate_full, out_full, gu_full, down_full = (
        lax.all_gather(w_qkv, ("shard", "ctx"), axis=0, tiled=True),
        lax.all_gather(w_forget, ("shard", "ctx"), axis=0, tiled=True),
        lax.all_gather(w_ogate, ("shard", "ctx"), axis=0, tiled=True),
        lax.all_gather(w_out, ("shard", "ctx"), axis=0, tiled=True),
        lax.all_gather(w_gu, ("shard", "ctx"), axis=0, tiled=True),
        lax.all_gather(w_down, ("shard", "ctx"), axis=0, tiled=True),
    )
    qkv_flat = qkv_full.reshape(model_width, 3 * head_cols)
    gu_flat = gu_full.reshape(model_width, 2 * hidden_units)

    def own_slice(values):
        return lax.dynamic_slice_in_dim(
            values.reshape(slot_count, half_rows, values.shape[-1]), own_start, own_rows, 1
        )

    positions = span_index * half_rows + jnp.arange(half_rows, dtype=jnp.int32)
    valid_rows = (positions[None, :] < lengths[:, None]).astype(jnp.float32).reshape(row_count, 1)
    own_positions = span_index * half_rows + own_start + jnp.arange(own_rows, dtype=jnp.int32)
    valid_own = (own_positions[None, :] < lengths[:, None]).astype(jnp.float32)[:, :, None]
    residual = full_tokens.reshape(row_count, model_width).astype(jnp.float32)
    normed = norm_rows(residual, gain_attn).astype(jnp.bfloat16)
    qkv_rows = product(normed, qkv_flat).reshape(row_count, 3, head_cols)
    query_raw = qkv_rows[:, 0].reshape(row_count, local_heads, head_size)
    key_raw = qkv_rows[:, 1].reshape(row_count, local_heads, head_size)
    queries = (
        norm_rows(query_raw, qk_gain[0])
        .astype(jnp.bfloat16)
        .reshape(slot_count, half_rows, head_cols)
    )
    keys_here = (
        norm_rows(key_raw, qk_gain[1])
        .astype(jnp.bfloat16)
        .reshape(slot_count, half_rows, head_cols)
    )
    values_here = qkv_rows[:, 2].astype(jnp.bfloat16).reshape(slot_count, half_rows, head_cols)
    bias_here = lax.dynamic_slice_in_dim(forget_bias, tensor_place * local_heads, local_heads)
    forget_pre = (product(normed, forget_full) + bias_here).reshape(
        slot_count, half_rows, local_heads
    )
    cum_here = jnp.cumsum(jax.nn.log_sigmoid(forget_pre), axis=1)
    keys_left, values_left = shifted((keys_here, values_here), "ctx", 1)
    cum_left = shifted(cum_here, "ctx", 1)
    cum_query = cum_here + cum_left[:, -1:, :]

    def by_head(values):
        shaped = values.reshape(slot_count, half_rows, local_heads, head_size)
        return jnp.transpose(shaped, (0, 2, 1, 3)).reshape(item_count, half_rows, head_size)

    def by_head_cum(values):
        return jnp.transpose(values, (0, 2, 1)).reshape(item_count, half_rows)

    def to_slots(values):
        shaped = values.reshape(slot_count, local_heads, half_rows, head_size)
        return jnp.transpose(shaped, (0, 2, 1, 3)).reshape(slot_count, half_rows, head_cols)

    def to_slots_cum(values):
        return jnp.transpose(values.reshape(slot_count, local_heads, half_rows), (0, 2, 1))

    q_items = by_head(queries)
    k_items = jnp.concatenate([by_head(keys_left), by_head(keys_here)], axis=1)
    v_items = jnp.concatenate([by_head(values_left), by_head(values_here)], axis=1)
    cq_items = by_head_cum(cum_query)
    ck_items = jnp.concatenate([by_head_cum(cum_left), cq_items], axis=1)
    place_ids = jnp.arange(half_rows, dtype=jnp.int32)
    earlier = jnp.broadcast_to(span_index > 0, (half_rows, half_rows))
    allowed = jnp.concatenate([earlier, place_ids[None, :] <= place_ids[:, None]], axis=1)

    def score_block(query_block, key_block, cum_rows, cum_cols):
        score_raw = (
            product_t(query_block, key_block) * score_scale + cum_rows[:, None] - cum_cols[None, :]
        )
        return jnp.where(allowed, score_raw, -jnp.inf)

    def forward_item(pieces):
        query_block, key_block, value_block, cum_rows, cum_cols = pieces
        score_vals = score_block(query_block, key_block, cum_rows, cum_cols)
        row_max = jnp.max(score_vals, axis=1, keepdims=True)
        expo = jnp.exp(score_vals - row_max)
        row_total = jnp.sum(expo, axis=1, keepdims=True)
        attn_probs = (expo / row_total).astype(jnp.bfloat16)
        return (product(attn_probs, value_block), (row_max + jnp.log(row_total))[:, 0])

    attended_items, lse_items = lax.map(
        forward_item, (q_items, k_items, v_items, cq_items, ck_items)
    )
    attended_rows = to_slots(attended_items).reshape(row_count, head_cols)
    opener = jax.nn.sigmoid(product(normed, ogate_full))
    gated = (attended_rows * opener).astype(jnp.bfloat16)
    branch_part = product_t(gated, out_full)
    branch_full = lax.psum(branch_part, "tp")
    middle = residual + branch_full
    middle_share = own_slice(middle)
    normed_mid = norm_rows(middle, gain_mlp).astype(jnp.bfloat16)
    both = product(normed_mid, gu_flat).reshape(row_count, 2, hidden_units)
    gate_pre = both[:, 0]
    up_pre = both[:, 1]
    gate_sig = jax.nn.sigmoid(gate_pre)
    hidden = (gate_pre * gate_sig * up_pre).astype(jnp.bfloat16)
    down_share = lax.psum_scatter(
        product_t(hidden, down_full)
        .reshape(slot_count, half_rows, model_width)
        .astype(jnp.bfloat16),
        "tp",
        scatter_dimension=1,
        tiled=True,
    ).astype(jnp.float32)
    output = (valid_own * (middle_share + down_share)).astype(jnp.bfloat16)
    cot_rows = full_cot.reshape(row_count, model_width) * valid_rows.astype(jnp.bfloat16)
    d_hidden = product(cot_rows, down_full)
    d_gate = d_hidden * up_pre * gate_sig * (1.0 + gate_pre * (1.0 - gate_sig))
    d_up = d_hidden * gate_pre * gate_sig
    d_both = (
        jnp.stack([d_gate, d_up], axis=1).astype(jnp.bfloat16).reshape(row_count, 2 * hidden_units)
    )
    grad_down = outer_rows(cot_rows, hidden)
    grad_gu = outer_rows(normed_mid, d_both).reshape(model_width, 2, hidden_units)
    d_mid_terms = product_t(d_both, gu_flat)
    d_normed_mid = lax.psum(d_mid_terms, "tp")
    _, pull_mid = jax.vjp(norm_rows, middle, gain_mlp)
    d_middle_norm, d_gain_mlp_all = pull_mid(d_normed_mid)
    d_middle = d_middle_norm + cot_rows.astype(jnp.float32)
    feat_share = model_width // tensor_size
    owner = jnp.arange(model_width, dtype=jnp.int32) // feat_share == tensor_place
    d_gain_mlp_own = jnp.where(owner, d_gain_mlp_all, 0.0)
    d_branch = d_middle.astype(jnp.bfloat16)
    d_middle_share = own_slice(d_middle)
    d_gated = product(d_branch, out_full)
    grad_out = outer_rows(d_branch, gated)
    d_attended = (d_gated * opener).astype(jnp.bfloat16)
    d_open = (d_gated * attended_rows * opener * (1.0 - opener)).astype(jnp.bfloat16)
    grad_ogate = outer_rows(normed, d_open)
    da_items = by_head(d_attended.reshape(slot_count, half_rows, head_cols))

    def backward_item(pieces):
        query_block, key_block, value_block, cum_rows, cum_cols, lse_block, grad_block = pieces
        score_vals = score_block(query_block, key_block, cum_rows, cum_cols)
        attn_probs = jnp.exp(score_vals - lse_block[:, None])
        d_probs = product_t(grad_block, value_block)
        centre = jnp.sum(attn_probs * d_probs, axis=1, keepdims=True)
        d_scores = (attn_probs * (d_probs - centre)).astype(jnp.bfloat16)
        d_query_block = product(d_scores, key_block) * score_scale
        d_key_block = outer_rows(d_scores, query_block) * score_scale
        d_value_block = outer_rows(attn_probs.astype(jnp.bfloat16), grad_block)
        d_cum_rows = jnp.sum(d_scores, axis=1, dtype=jnp.float32)
        d_cum_cols = -jnp.sum(d_scores, axis=0, dtype=jnp.float32)
        return (d_query_block, d_key_block, d_value_block, d_cum_rows, d_cum_cols)

    dq_items, dk_items, dv_items, dcq_items, dck_items = lax.map(
        backward_item, (q_items, k_items, v_items, cq_items, ck_items, lse_items, da_items)
    )
    dc_own = dcq_items + dck_items[:, half_rows:]
    dc_left = dck_items[:, :half_rows]
    dc_left = dc_left.at[:, -1].add(jnp.sum(dc_own, axis=1))
    back_keys, back_values, back_cum = (
        shifted(to_slots(dk_items[:, :half_rows]).astype(jnp.bfloat16), "ctx", -1).astype(
            jnp.float32
        ),
        shifted(to_slots(dv_items[:, :half_rows]).astype(jnp.bfloat16), "ctx", -1).astype(
            jnp.float32
        ),
        shifted(to_slots_cum(dc_left).astype(jnp.bfloat16), "ctx", -1).astype(jnp.float32),
    )
    d_query = to_slots(dq_items).reshape(row_count, local_heads, head_size)
    d_key = (to_slots(dk_items[:, half_rows:]) + back_keys).reshape(
        row_count, local_heads, head_size
    )
    d_value = (to_slots(dv_items[:, half_rows:]) + back_values).reshape(row_count, head_cols)
    d_cum = to_slots_cum(dc_own) + back_cum
    d_log = jnp.flip(jnp.cumsum(jnp.flip(d_cum, 1), axis=1), 1)
    d_forget = d_log * jax.nn.sigmoid(-forget_pre)
    d_bias_own = jnp.sum(d_forget, axis=(0, 1))
    d_forget_low = d_forget.reshape(row_count, local_heads).astype(jnp.bfloat16)
    grad_forget = outer_rows(normed, d_forget_low)
    _, pull_query = jax.vjp(norm_rows, query_raw, qk_gain[0])
    d_query_raw, d_query_gain = pull_query(d_query)
    _, pull_key = jax.vjp(norm_rows, key_raw, qk_gain[1])
    d_key_raw, d_key_gain = pull_key(d_key)
    d_mixed = (
        jnp.stack(
            [
                d_query_raw.reshape(row_count, head_cols),
                d_key_raw.reshape(row_count, head_cols),
                d_value,
            ],
            axis=1,
        )
        .astype(jnp.bfloat16)
        .reshape(row_count, 3 * head_cols)
    )
    grad_qkv = outer_rows(normed, d_mixed).reshape(model_width, 3, head_cols)
    d_normed = (
        product_t(d_mixed, qkv_flat)
        + product_t(d_open, ogate_full)
        + product_t(d_forget_low, forget_full)
    )
    root = lax.rsqrt(jnp.mean(residual * residual, axis=1, keepdims=True) + epsilon)
    unit = residual * root
    d_unit = d_normed * gain_attn
    dot_part = (jnp.sum(d_unit * unit, axis=1) / model_width).reshape(slot_count, half_rows)
    d_unit_share, dot_full = (
        lax.psum_scatter(
            d_unit.reshape(slot_count, half_rows, model_width).astype(jnp.bfloat16),
            "tp",
            scatter_dimension=1,
            tiled=True,
        ).astype(jnp.float32),
        lax.psum_scatter(
            dot_part.astype(jnp.bfloat16), "tp", scatter_dimension=1, tiled=True
        ).astype(jnp.float32),
    )
    unit_share = own_slice(unit)
    root_share = own_slice(root)
    input_grad = (
        d_middle_share + root_share * (d_unit_share - unit_share * dot_full[:, :, None])
    ).astype(jnp.bfloat16)
    grad_parts = (
        lax.psum_scatter(
            grad_qkv.astype(jnp.bfloat16), ("shard", "ctx"), scatter_dimension=0, tiled=True
        ).astype(jnp.float32),
        lax.psum_scatter(
            grad_forget.astype(jnp.bfloat16), ("shard", "ctx"), scatter_dimension=0, tiled=True
        ).astype(jnp.float32),
        lax.psum_scatter(
            grad_ogate.astype(jnp.bfloat16), ("shard", "ctx"), scatter_dimension=0, tiled=True
        ).astype(jnp.float32),
        lax.psum_scatter(
            grad_out.astype(jnp.bfloat16), ("shard", "ctx"), scatter_dimension=0, tiled=True
        ).astype(jnp.float32),
        lax.psum_scatter(
            grad_gu.astype(jnp.bfloat16), ("shard", "ctx"), scatter_dimension=0, tiled=True
        ).astype(jnp.float32),
        lax.psum_scatter(
            grad_down.astype(jnp.bfloat16), ("shard", "ctx"), scatter_dimension=0, tiled=True
        ).astype(jnp.float32),
    )
    bias_full = lax.dynamic_update_slice_in_dim(
        jnp.zeros(forget_bias.shape, jnp.float32), d_bias_own, tensor_place * local_heads, 0
    )
    gain_attn_part = jnp.sum(d_normed * unit, axis=0)
    small_parts = lax.psum(
        (gain_attn_part, d_gain_mlp_own, jnp.stack([d_query_gain, d_key_gain]), bias_full),
        ("shard", "ctx", "tp"),
    )
    return (
        output,
        input_grad,
        grad_parts[0],
        grad_parts[1],
        small_parts[3],
        grad_parts[2],
        grad_parts[3],
        grad_parts[4],
        grad_parts[5],
        small_parts[0],
        small_parts[1],
        small_parts[2],
    )


def solution(mesh):
    return jax.shard_map(
        body,
        mesh=mesh,
        in_specs=(
            P("shard", ("ctx", "tp"), None),
            P("shard", ("ctx", "tp"), None),
            P("shard"),
            P(("shard", "ctx"), None, "tp"),
            P(("shard", "ctx"), "tp"),
            P(),
            P(("shard", "ctx"), "tp"),
            P(("shard", "ctx"), "tp"),
            P(("shard", "ctx"), None, "tp"),
            P(("shard", "ctx"), "tp"),
            P(),
            P(),
            P(),
        ),
        out_specs=(
            P("shard", ("ctx", "tp"), None),
            P("shard", ("ctx", "tp"), None),
            P(("shard", "ctx"), None, "tp"),
            P(("shard", "ctx"), "tp"),
            P(),
            P(("shard", "ctx"), "tp"),
            P(("shard", "ctx"), "tp"),
            P(("shard", "ctx"), None, "tp"),
            P(("shard", "ctx"), "tp"),
            P(),
            P(),
            P(),
        ),
        check_vma=False,
    )
```

profile of v0, /device:TPU:0, one launch (start us, length us, event | category | flops | bytes accessed | tf_op | source)
XLA Modules:
  0.0 1049.7 jit_solution(11627350117377922482)
XLA Ops:
  11.9 10.6 %all-gather = bf16[8,192,6]{1,2,0:T(8,128)(2,1)S(1)} all-gather(bf16[1,192,6]{1,2,0:T(8,128)(2,1)} %bitcast.510), channel_id=1, replica_groups=mesh['shard'=4,'ctx'=2,'tp'=4] {'shard','ctx'}, dimensions={0}, use_global_device_ids=true | all-gather | bytes 20736 | tf_op jit(solution)/shard_map/all_gather | solution.py:70
  24.6 24.8 %all-gather.9.cloned.1.call-done = bf16[1,512,1536]{2,1,0:T(8,128)(2,1)} async-done(((bf16[1,128,1536]{2,1,0:T(8,128)(2,1)}), bf16[1,512,1536]{2,1,0:T(8,128)(2,1)}) %all-gather.9.cloned.1.call-update) | async-done | bytes 1572880 | tf_op jit(solution)/shard_map/all_gather | solution.py:65
  59.5 24.7 %all-gather.11.cloned.1.call-done = bf16[1536,3,384]{2,0,1:T(8,128)(2,1)} async-done(((bf16[192,3,384]{2,0,1:T(8,128)(2,1)}), bf16[1536,3,384]{2,0,1:T(8,128)(2,1)}) %all-gather.11.cloned.1.call-update) | async-done | bytes 3538960 | tf_op jit(solution)/shard_map/all_gather | solution.py:69
  84.2 6.1 copy.92
  118.7 37.0 %while.31 = (s32[]{:T(128)}, f32[6,512,64]{1,2,0:T(8,128)}, f32[6,512]{1,0:T(8,128)S(1)}, bf16[6,512,64]{2,1,0:T(8,128)(2,1)}, bf16[6,1024,64]{2,1,0:T(8,128)(2,...) while((s32[]{:T(128)}, f32[6,512,64]{1,2,0:T(8,128)}, ...), condition=%wide.region_8.9_spmd, body=%wide.region_5.8_spmd.sunk | while | flops 139460096 | bytes 7643265 | solution.py:151
  168.9 116.0 %all-reduce.5.cloned.1.call-done = f32[512,1536]{1,0:T(8,128)} async-done(((f32[512,1536]{1,0:T(8,128)}), f32[512,1536]{1,0:T(8,128)}) %all-reduce.5.cloned.1.call-update) | async-done | bytes 3145744 | tf_op jit(solution)/shard_map/psum | solution.py:158
  289.3 42.5 %all-gather.17.cloned.1.call-done = bf16[1536,2,1024]{2,0,1:T(8,128)(2,1)} async-done(((bf16[192,2,1024]{2,0,1:T(8,128)(2,1)}), bf16[1536,2,1024]{2,0,1:T(8,128)(2,1)}) %all-gather.17.cloned.1.call-update) | async-done | bytes 6291472 | tf_op jit(solution)/shard_map/all_gather | solution.py:73
  331.8 8.7 copy.104
  340.5 8.1 fusion.36
  348.6 21.9 %all-gather.21.cloned.1.call-done = bf16[1,512,1536]{2,1,0:T(8,128)(2,1)} async-done(((bf16[1,128,1536]{2,1,0:T(8,128)(2,1)}), bf16[1,512,1536]{2,1,0:T(8,128)(2,1)}) %all-gather.21.cloned.1.call-update) | async-done | bytes 1572880 | tf_op jit(solution)/shard_map/all_gather | solution.py:66
  370.5 33.1 %all-gather.19.cloned.1.call-done = bf16[1536,1024]{1,0:T(8,128)(2,1)} async-done(((bf16[192,1024]{1,0:T(8,128)(2,1)}), bf16[1536,1024]{1,0:T(8,128)(2,1)}) %all-gather.19.cloned.1.call-update) | async-done | bytes 3145744 | tf_op jit(solution)/shard_map/all_gather | solution.py:74
  410.9 8.0 convolution_bitcast_fusion.2
  423.5 6.7 fusion.47
  430.5 109.7 %all-reduce.7.cloned.1.call-done = f32[512,1536]{1,0:T(8,128)} async-done(((f32[512,1536]{1,0:T(8,128)}), f32[512,1536]{1,0:T(8,128)}) %all-reduce.7.cloned.1.call-update) | async-done | bytes 3145744 | tf_op jit(solution)/shard_map/psum | solution.py:186
  552.2 97.2 %while.32 = (s32[]{:T(128)}, f32[6,512,64]{1,2,0:T(8,128)}, f32[6,1024,64]{1,2,0:T(8,128)}, f32[6,1024,64]{1,2,0:T(8,128)}, f32[6,512]{1,0:T(8,128)}, /*index=5*...) while((s32[]{:T(128)}, f32[6,512,64]{1,2,0:T(8,128)}, ...), condition=%wide.region_18.19_spmd, body=%wide.region_14.18_spmd.sunk | while | flops 342981632 | bytes 20376776 | solution.py:216
  715.7 6.4 convolution_convert_fusion.2
  742.0 8.9 convolution_convert_fusion
  755.5 41.1 %all-reduce.1 = (f32[24]{0:T(128)}, f32[1536]{0:T(1024)}, f32[1536]{0:T(1024)}, f32[2,64]{1,0:T(2,128)}) all-reduce(f32[24]{0:T(128)S(1)} %dynamic_update_slice.28, f32[1536]{0:T(1024)S(1)} %get-tuple-element.207, f32[1536]{0:T(1024)S(1)} %fusion.108, ...), channel_id=1, replica_groups=mesh['shard'=4,'ctx'=2,'tp'=4] {'shard','ctx','tp'}, use_global_device_ids=true, to_apply=%region_30.31 | all-reduce | flops 3224 | bytes 25792 | tf_op jit(solution)/shard_map/psum | solution.py:308
  797.5 8.2 reduce-scatter.26.cloned.1.call-done
  807.7 37.9 %reduce-scatter.20.cloned.1.call-done = bf16[192,384]{1,0:T(8,128)(2,1)} async-done(((bf16[1536,384]{1,0:T(8,128)(2,1)}), bf16[192,384]{1,0:T(8,128)(2,1)}) %reduce-scatter.20.cloned.1.call-update) | async-done | bytes 147472 | tf_op jit(solution)/shard_map/reduce_scatter | solution.py:291
  847.2 38.6 %reduce-scatter.22.cloned.1.call-done = bf16[192,384]{1,0:T(8,128)(2,1)} async-done(((bf16[1536,384]{1,0:T(8,128)(2,1)}), bf16[192,384]{1,0:T(8,128)(2,1)}) %reduce-scatter.22.cloned.1.call-update) | async-done | bytes 147472 | tf_op jit(solution)/shard_map/reduce_scatter | solution.py:294
  887.5 36.4 %reduce-scatter.16.cloned.1.call-done = bf16[1,128,1536]{2,1,0:T(8,128)(2,1)} async-done(((bf16[1,512,1536]{2,1,0:T(8,128)(2,1)}), bf16[1,128,1536]{2,1,0:T(8,128)(2,1)}) %reduce-scatter.16.cloned.1.call-update) | async-done | bytes 393232 | tf_op jit(solution)/shard_map/reduce_scatter | solution.py:269
  926.1 48.2 %reduce-scatter.18.cloned.1.call-done = bf16[192,3,384]{2,0,1:T(8,128)(2,1)} async-done(((bf16[1536,3,384]{2,0,1:T(8,128)(2,1)}), bf16[192,3,384]{2,0,1:T(8,128)(2,1)}) %reduce-scatter.18.cloned.1.call-update) | async-done | bytes 442384 | tf_op jit(solution)/shard_map/reduce_scatter | solution.py:285
  976.3 63.0 %reduce-scatter.24.cloned.1.call-done = bf16[192,2,1024]{2,0,1:T(8,128)(2,1)} async-done(((bf16[1536,2,1024]{2,0,1:T(8,128)(2,1)}), bf16[192,2,1024]{2,0,1:T(8,128)(2,1)}) %reduce-scatter.24.cloned.1.call-update) | async-done | bytes 786448 | tf_op jit(solution)/shard_map/reduce_scatter | solution.py:297
  (443 shorter events, 323.4 us)
Async XLA Ops:
  7.2 42.2 %all-gather.9.cloned.1.call-start = ((), (), s32[]{:S(2)}) async-start(), calls=%async_computation.9 | async-start | bytes 1966080 | tf_op jit(solution)/shard_map/all_gather | solution.py:65
  7.9 76.3 %all-gather.11.cloned.1.call-start = ((), (), s32[]{:S(2)}) async-start(), calls=%async_computation.10 | async-start | bytes 3981312 | tf_op jit(solution)/shard_map/all_gather | solution.py:69
  8.7 147.0 %all-gather.13.cloned.1.call-start = ((), (), s32[]{:S(2)}) async-start(), calls=%async_computation.11 | async-start | bytes 1327104 | tf_op jit(solution)/shard_map/all_gather | solution.py:71
  9.4 150.3 %all-gather.15.cloned.1.call-start = ((), (), s32[]{:S(2)}) async-start(), calls=%async_computation.12 | async-start | bytes 1327104 | tf_op jit(solution)/shard_map/all_gather | solution.py:72
  10.0 274.9 %all-reduce.5.cloned.1.call-start = ((), (), s32[]{:S(2)}) async-start(), calls=%async_computation.13 | async-start | bytes 6291456 | tf_op jit(solution)/shard_map/psum | solution.py:158
  55.5 2.4 collective-permute-start.1
  96.7 13.4 %collective-permute-start = (bf16[1,512,384]{1,2,0:T(8,128)(2,1)}, bf16[1,512,384]{1,2,0:T(8,128)(2,1)}, u32[]{:S(2)}, u32[]{:S(2)}) collective-permute-start(bf16[1,512,384]{1,2,0:T(8,128)(2,1)} %multiply_convert_fusion.9), channel_id=1, source_target_pairs={{0,4},{1,5},{2,6},{3,7},{8,12},{9,13},{10,14},{11,15},{16,20},{17,... | collective-permute-start | bytes 1179656 | tf_op jit(solution)/shard_map/ppermute | solution.py:13
  99.6 12.7 %collective-permute-start.2 = (bf16[1,512,384]{1,2,0:T(8,128)(2,1)}, bf16[1,512,384]{1,2,0:T(8,128)(2,1)}, u32[]{:S(2)}, u32[]{:S(2)}) collective-permute-start(bf16[1,512,384]{1,2,0:T(8,128)(2,1)} %slice_bitcast_fusion.5), channel_id=1, source_target_pairs={{0,4},{1,5},{2,6},{3,7},{8,12},{9,13},{10,14},{11,15},{16,20},{17,... | collective-permute-start | bytes 1179656 | tf_op jit(solution)/shard_map/ppermute | solution.py:13
  163.7 168.1 %all-gather.17.cloned.1.call-start = ((), (), s32[]{:S(2)}) async-start(), calls=%async_computation.14 | async-start | bytes 7077888 | tf_op jit(solution)/shard_map/all_gather | solution.py:73
  165.9 204.6 %all-gather.21.cloned.1.call-start = ((), (), s32[]{:S(2)}) async-start(), calls=%async_computation.17 | async-start | bytes 1966080 | tf_op jit(solution)/shard_map/all_gather | solution.py:66
  166.7 236.9 %all-gather.19.cloned.1.call-start = ((), (), s32[]{:S(2)}) async-start(), calls=%async_computation.15 | async-start | bytes 3538944 | tf_op jit(solution)/shard_map/all_gather | solution.py:74
  167.4 372.7 %all-reduce.7.cloned.1.call-start = ((), (), s32[]{:S(2)}) async-start(), calls=%async_computation.18 | async-start | bytes 6291456 | tf_op jit(solution)/shard_map/psum | solution.py:186
  418.9 332.6 %reduce-scatter.14.cloned.1.call-start = ((), (), s32[]{:S(2)}) async-start(), calls=%async_computation.16 | async-start | bytes 1966080 | tf_op jit(solution)/shard_map/reduce_scatter | solution.py:167
  430.2 323.7 %reduce-scatter.30.cloned.1.call-start = ((), (), s32[]{:S(2)}) async-start(), calls=%async_computation.26 | async-start | bytes 442368
  653.4 51.8 %collective-permute-start.4 = (bf16[1,512,384]{1,2,0:T(8,128)(2,1)}, bf16[1,512,384]{1,2,0:T(8,128)(2,1)}, u32[]{:S(2)}, u32[]{:S(2)}) collective-permute-start(bf16[1,512,384]{1,2,0:T(8,128)(2,1)} %bitcast.100), channel_id=1, source_target_pairs={{4,0},{5,1},{6,2},{7,3},{12,8},{13,9},{14,10},{15,11},{20,16},{21,... | collective-permute-start | bytes 1179656 | tf_op jit(solution)/shard_map/ppermute | solution.py:13
  656.6 44.0 %collective-permute-start.3 = (bf16[1,512,384]{1,2,0:T(8,128)(2,1)}, bf16[1,512,384]{1,2,0:T(8,128)(2,1)}, u32[]{:S(2)}, u32[]{:S(2)}) collective-permute-start(bf16[1,512,384]{1,2,0:T(8,128)(2,1)} %bitcast.90), channel_id=1, source_target_pairs={{4,0},{5,1},{6,2},{7,3},{12,8},{13,9},{14,10},{15,11},{20,16},{21,... | collective-permute-start | bytes 1179656 | tf_op jit(solution)/shard_map/ppermute | solution.py:13
  665.8 6.0 collective-permute-start.5
  700.3 96.4 %reduce-scatter.28.cloned.1.call-start = ((), (), s32[]{:S(2)}) async-start(), calls=%async_computation.25 | async-start | bytes 163840
  715.7 90.0 %reduce-scatter.26.cloned.1.call-start = ((), (), s32[]{:S(2)}) async-start(), calls=%async_computation.24 | async-start | bytes 3538944 | tf_op jit(solution)/shard_map/reduce_scatter | solution.py:300
  722.2 123.4 %reduce-scatter.20.cloned.1.call-start = ((), (), s32[]{:S(2)}) async-start(), calls=%async_computation.21 | async-start | bytes 1327104 | tf_op jit(solution)/shard_map/reduce_scatter | solution.py:291
  725.9 159.9 %reduce-scatter.22.cloned.1.call-start = ((), (), s32[]{:S(2)}) async-start(), calls=%async_computation.22 | async-start | bytes 1327104 | tf_op jit(solution)/shard_map/reduce_scatter | solution.py:294
  728.0 195.8 %reduce-scatter.16.cloned.1.call-start = ((), (), s32[]{:S(2)}) async-start(), calls=%async_computation.19 | async-start | bytes 1966080 | tf_op jit(solution)/shard_map/reduce_scatter | solution.py:269
  728.6 245.7 %reduce-scatter.18.cloned.1.call-start = ((), (), s32[]{:S(2)}) async-start(), calls=%async_computation.20 | async-start | bytes 3981312 | tf_op jit(solution)/shard_map/reduce_scatter | solution.py:285
  734.9 304.4 %reduce-scatter.24.cloned.1.call-start = ((), (), s32[]{:S(2)}) async-start(), calls=%async_computation.23 | async-start | bytes 7077888 | tf_op jit(solution)/shard_map/reduce_scatter | solution.py:297
  (75 other events, 701.1 us)
Sparse Core Ops, SparseCore 0:
  9.6 39.7 all-gather.8
  51.3 32.8 all-gather.10
  86.1 24.0 all-gather.12
  112.0 24.0 all-gather.14
  163.8 121.0 all-reduce.4
  287.2 44.5 all-gather.16
  333.4 37.0 all-gather.20
  372.4 31.1 all-gather.18
  419.0 121.0 all-reduce.6
  542.3 34.2 reduce-scatter.13
  700.4 35.1 reduce-scatter.29
  738.2 19.1 reduce-scatter.27
  761.2 44.4 reduce-scatter.25
  808.8 36.7 reduce-scatter.19
  849.0 36.7 reduce-scatter.21
  888.6 35.2 reduce-scatter.15
  927.2 47.0 reduce-scatter.17
  977.5 61.7 reduce-scatter.23
where the time goes:
time: 1060 us; the launch traced here: 1050 us
  waiting for transfers between devices  611 us (58%)
  matrix products  162 us (15%)
  local copies, waits for them, and re-layouts  121 us (11%)
  other arithmetic  75.4 us (7%)
  blocking collectives  51.8 us (5%)
  between operations  16.4 us (2%)
  starting transfers between devices  12.2 us (1%)
    psum x1, waiting for transfers between devices, body(): branch_full = lax.psum(branch_part, 'tp')  116 us
    psum x1, waiting for transfers between devices, body(): d_normed_mid = lax.psum(d_mid_terms, 'tp')  110 us
    reduce_scatter x1, waiting for transfers between devices, body(): lax.psum_scatter(grad_gu.astype(jnp.bfloat16), ('shard', 'ctx'), scatter_...  63 us
    dot_general x24, matrix products, product_t(): lax.dot_general(left, right, (((1,), (1,)), ((), ())), preferred_element_...  58 us
    dot_general x18, matrix products, outer_rows(): lax.dot_general(left, right, (((0,), (0,)), ((), ())), preferred_element_...  52.8 us
    dot_general x18, matrix products, product(): return jnp.dot(left, right, preferred_element_type=jnp.float32)  51.2 us
    reduce_scatter x1, waiting for transfers between devices, body(): lax.psum_scatter(grad_qkv.astype(jnp.bfloat16), ('shard', 'ctx'), scatter...  48.2 us
    all_gather x1, waiting for transfers between devices, body(): lax.all_gather(w_gu, ('shard', 'ctx'), axis=0, tiled=True)  42.5 us
  transfers between devices with their start and end apart: 24, of which 14 were waited for; matrix products, arithmetic and copies ran while one was open for 31% of the time, Pallas kernels for 0%

commit v1 on v0

--- a/solution.py
+++ b/solution.py
@@ -183,7 +183,11 @@
     grad_down = outer_rows(cot_rows, hidden)
     grad_gu = outer_rows(normed_mid, d_both).reshape(model_width, 2, hidden_units)
     d_mid_terms = product_t(d_both, gu_flat)
-    d_normed_mid = lax.psum(d_mid_terms, "tp")
+    d_normed_mid = d_mid_terms
+    for hop in (1, 2):
+        d_normed_mid = d_normed_mid + lax.ppermute(
+            d_normed_mid, "tp", [(dev, dev ^ hop) for dev in range(4)]
+        )
     _, pull_mid = jax.vjp(norm_rows, middle, gain_mlp)
     d_middle_norm, d_gain_mlp_all = pull_mid(d_normed_mid)
     d_middle = d_middle_norm + cot_rows.astype(jnp.float32)

time: 1060 us -> 1130 us (1.066)
  waiting for transfers between devices: 611 us -> 674 us
    ppermute x0 -> x2, waiting for transfers between devices: none -> 216 us  [body(): lax.ppermute(d_normed_mid, 'tp', [(dev, dev ^ hop) for dev in range(4)])]
    psum x1 -> x0, waiting for transfers between devices: 110 us -> none  [body(): d_normed_mid = lax.psum(d_mid_terms, 'tp')]
    reduce_scatter x1, waiting for transfers between devices: 37.9 us -> 4.5 us  [body(): lax.psum_scatter(grad_ogate.astype(jnp.bfloat16), ('shard', 'ctx'), scatt...]
  transfers between devices with their start and end apart: 24 -> 25, of which waited for: 14 -> 14; matrix products, arithmetic and copies ran while one was open for 31% -> 30% of each run, Pallas kernels for 0% -> 0%
where the time goes in v1:
time: 1130 us; the launch traced here: 1120 us
  waiting for transfers between devices  674 us (60%)
  matrix products  160 us (14%)
  local copies, waits for them, and re-layouts  120 us (11%)
  other arithmetic  82.1 us (7%)
  blocking collectives  51.9 us (5%)
  starting transfers between devices  16.1 us (1%)
  between operations  16 us (1%)
    ppermute x2, waiting for transfers between devices, body(): lax.ppermute(d_normed_mid, 'tp', [(dev, dev ^ hop) for dev in range(4)])  216 us
    psum x1, waiting for transfers between devices, body(): branch_full = lax.psum(branch_part, 'tp')  116 us
    reduce_scatter x1, waiting for transfers between devices, body(): lax.psum_scatter(grad_gu.astype(jnp.bfloat16), ('shard', 'ctx'), scatter_...  63.4 us
    dot_general x24, matrix products, product_t(): lax.dot_general(left, right, (((1,), (1,)), ((), ())), preferred_element_...  55.1 us
    dot_general x18, matrix products, outer_rows(): lax.dot_general(left, right, (((0,), (0,)), ((), ())), preferred_element_...  53.4 us
    dot_general x18, matrix products, product(): return jnp.dot(left, right, preferred_element_type=jnp.float32)  51.3 us
    reduce_scatter x1, waiting for transfers between devices, body(): lax.psum_scatter(grad_qkv.astype(jnp.bfloat16), ('shard', 'ctx'), scatter...  48.4 us
    all_gather x1, waiting for transfers between devices, body(): lax.all_gather(w_gu, ('shard', 'ctx'), axis=0, tiled=True)  42.9 us
  transfers between devices with their start and end apart: 25, of which 14 were waited for; matrix products, arithmetic and copies ran while one was open for 30% of the time, Pallas kernels for 0%

profile of v1, /device:TPU:0, one launch (start us, length us, event | category | flops | bytes accessed | tf_op | source)
XLA Modules:
  0.0 1119.6 jit_solution(7039860153011921604)
XLA Ops:
  12.0 10.6 all-gather
  24.8 24.6 %all-gather.9.cloned.1.call-done = bf16[1,512,1536]{2,1,0:T(8,128)(2,1)} async-done(((bf16[1,128,1536]{2,1,0:T(8,128)(2,1)}), bf16[1,512,1536]{2,1,0:T(8,128)(2,1)}) %all-gather.9.cloned.1.call-update) | async-done | bytes 1572880 | tf_op jit(solution)/shard_map/all_gather | solution.py:65
  59.5 24.7 %all-gather.11.cloned.1.call-done = bf16[1536,3,384]{2,0,1:T(8,128)(2,1)} async-done(((bf16[192,3,384]{2,0,1:T(8,128)(2,1)}), bf16[1536,3,384]{2,0,1:T(8,128)(2,1)}) %all-gather.11.cloned.1.call-update) | async-done | bytes 3538960 | tf_op jit(solution)/shard_map/all_gather | solution.py:69
  84.2 6.1 copy.92
  118.7 37.0 %while.31 = (s32[]{:T(128)}, f32[6,512,64]{1,2,0:T(8,128)}, f32[6,512]{1,0:T(8,128)S(1)}, bf16[6,512,64]{2,1,0:T(8,128)(2,1)}, bf16[6,1024,64]{2,1,0:T(8,128)(2,...) while((s32[]{:T(128)}, f32[6,512,64]{1,2,0:T(8,128)}, ...), condition=%wide.region_8.9_spmd, body=%wide.region_5.8_spmd.sunk | while | flops 139460096 | bytes 7643265 | solution.py:151
  168.9 116.1 %all-reduce.4.cloned.1.call-done = f32[512,1536]{1,0:T(8,128)} async-done(((f32[512,1536]{1,0:T(8,128)}), f32[512,1536]{1,0:T(8,128)}) %all-reduce.4.cloned.1.call-update) | async-done | bytes 3145744 | tf_op jit(solution)/shard_map/psum | solution.py:158
  289.0 42.9 %all-gather.17.cloned.1.call-done = bf16[1536,2,1024]{2,0,1:T(8,128)(2,1)} async-done(((bf16[192,2,1024]{2,0,1:T(8,128)(2,1)}), bf16[1536,2,1024]{2,0,1:T(8,128)(2,1)}) %all-gather.17.cloned.1.call-update) | async-done | bytes 6291472 | tf_op jit(solution)/shard_map/all_gather | solution.py:73
  331.9 8.7 copy.104
  340.6 8.1 fusion.36
  348.6 22.0 %all-gather.21.cloned.1.call-done = bf16[1,512,1536]{2,1,0:T(8,128)(2,1)} async-done(((bf16[1,128,1536]{2,1,0:T(8,128)(2,1)}), bf16[1,512,1536]{2,1,0:T(8,128)(2,1)}) %all-gather.21.cloned.1.call-update) | async-done | bytes 1572880 | tf_op jit(solution)/shard_map/all_gather | solution.py:66
  370.6 33.1 %all-gather.19.cloned.1.call-done = bf16[1536,1024]{1,0:T(8,128)(2,1)} async-done(((bf16[192,1024]{1,0:T(8,128)(2,1)}), bf16[1536,1024]{1,0:T(8,128)(2,1)}) %all-gather.19.cloned.1.call-update) | async-done | bytes 3145744 | tf_op jit(solution)/shard_map/all_gather | solution.py:74
  403.7 6.0 fusion.52
  409.7 8.8 convolution_bitcast_fusion.2
  423.1 91.3 %collective-permute-done.3 = f32[512,1536]{1,0:T(8,128)} collective-permute-done((f32[512,1536]{1,0:T(8,128)}, f32[512,1536]{1,0:T(8,128)}, u32[]{:S(2)}, u32[]{:S(2)}) %collective-permute-start.3) | collective-permute-done | bytes 3145760 | tf_op jit(solution)/shard_map/ppermute | solution.py:188
  526.5 6.4 convolution_convert_fusion.2
  533.2 124.4 %collective-permute-done.4 = f32[512,1536]{1,0:T(8,128)} collective-permute-done((f32[512,1536]{1,0:T(8,128)}, f32[512,1536]{1,0:T(8,128)}, u32[]{:S(2)}, u32[]{:S(2)}) %collective-permute-start.4) | collective-permute-done | bytes 3145760 | tf_op jit(solution)/shard_map/ppermute | solution.py:188
  671.7 97.3 %while.32 = (s32[]{:T(128)}, f32[6,512,64]{1,2,0:T(8,128)}, f32[6,1024,64]{1,2,0:T(8,128)}, f32[6,1024,64]{1,2,0:T(8,128)}, f32[6,512]{1,0:T(8,128)}, /*index=5*...) while((s32[]{:T(128)}, f32[6,512,64]{1,2,0:T(8,128)}, ...), condition=%wide.region_17.18_spmd, body=%wide.region_13.17_spmd.sunk | while | flops 342981632 | bytes 20376776 | solution.py:220
  850.2 7.5 convolution_convert_fusion
  858.7 5.8 convolution_convert_fusion.1
  870.4 41.2 %all-reduce.1 = (f32[24]{0:T(128)}, f32[1536]{0:T(1024)}, f32[1536]{0:T(1024)}, f32[2,64]{1,0:T(2,128)}) all-reduce(f32[24]{0:T(128)S(1)} %dynamic_update_slice.28, f32[1536]{0:T(1024)S(1)} %get-tuple-element.207, f32[1536]{0:T(1024)S(1)} %fusion.108, ...), channel_id=1, replica_groups=mesh['shard'=4,'ctx'=2,'tp'=4] {'shard','ctx','tp'}, use_global_device_ids=true, to_apply=%region_29.30 | all-reduce | flops 3224 | bytes 25792 | tf_op jit(solution)/shard_map/psum | solution.py:312
  918.6 38.6 %reduce-scatter.22.cloned.1.call-done = bf16[192,384]{1,0:T(8,128)(2,1)} async-done(((bf16[1536,384]{1,0:T(8,128)(2,1)}), bf16[192,384]{1,0:T(8,128)(2,1)}) %reduce-scatter.22.cloned.1.call-update) | async-done | bytes 147472 | tf_op jit(solution)/shard_map/reduce_scatter | solution.py:298
  958.8 63.4 %reduce-scatter.24.cloned.1.call-done = bf16[192,2,1024]{2,0,1:T(8,128)(2,1)} async-done(((bf16[1536,2,1024]{2,0,1:T(8,128)(2,1)}), bf16[192,2,1024]{2,0,1:T(8,128)(2,1)}) %reduce-scatter.24.cloned.1.call-update) | async-done | bytes 786448 | tf_op jit(solution)/shard_map/reduce_scatter | solution.py:301
  1025.3 34.5 %reduce-scatter.16.cloned.1.call-done = bf16[1,128,1536]{2,1,0:T(8,128)(2,1)} async-done(((bf16[1,512,1536]{2,1,0:T(8,128)(2,1)}), bf16[1,128,1536]{2,1,0:T(8,128)(2,1)}) %reduce-scatter.16.cloned.1.call-update) | async-done | bytes 393232 | tf_op jit(solution)/shard_map/reduce_scatter | solution.py:273
  1062.2 48.4 %reduce-scatter.18.cloned.1.call-done = bf16[192,3,384]{2,0,1:T(8,128)(2,1)} async-done(((bf16[1536,3,384]{2,0,1:T(8,128)(2,1)}), bf16[192,3,384]{2,0,1:T(8,128)(2,1)}) %reduce-scatter.18.cloned.1.call-update) | async-done | bytes 442384 | tf_op jit(solution)/shard_map/reduce_scatter | solution.py:289
  (445 shorter events, 330.3 us)
Async XLA Ops:
  7.2 42.2 %all-gather.9.cloned.1.call-start = ((), (), s32[]{:S(2)}) async-start(), calls=%async_computation.9 | async-start | bytes 1966080 | tf_op jit(solution)/shard_map/all_gather | solution.py:65
  7.9 76.3 %all-gather.11.cloned.1.call-start = ((), (), s32[]{:S(2)}) async-start(), calls=%async_computation.10 | async-start | bytes 3981312 | tf_op jit(solution)/shard_map/all_gather | solution.py:69
  8.7 147.1 %all-gather.13.cloned.1.call-start = ((), (), s32[]{:S(2)}) async-start(), calls=%async_computation.11 | async-start | bytes 1327104 | tf_op jit(solution)/shard_map/all_gather | solution.py:71
  9.4 150.3 %all-gather.15.cloned.1.call-start = ((), (), s32[]{:S(2)}) async-start(), calls=%async_computation.12 | async-start | bytes 1327104 | tf_op jit(solution)/shard_map/all_gather | solution.py:72
  10.0 275.0 %all-reduce.4.cloned.1.call-start = ((), (), s32[]{:S(2)}) async-start(), calls=%async_computation.13 | async-start | bytes 6291456 | tf_op jit(solution)/shard_map/psum | solution.py:158
  96.8 13.4 %collective-permute-start = (bf16[1,512,384]{1,2,0:T(8,128)(2,1)}, bf16[1,512,384]{1,2,0:T(8,128)(2,1)}, u32[]{:S(2)}, u32[]{:S(2)}) collective-permute-start(bf16[1,512,384]{1,2,0:T(8,128)(2,1)} %multiply_convert_fusion.9), channel_id=1, source_target_pairs={{0,4},{1,5},{2,6},{3,7},{8,12},{9,13},{10,14},{11,15},{16,20},{17,... | collective-permute-start | bytes 1179656 | tf_op jit(solution)/shard_map/ppermute | solution.py:13
  99.7 12.7 %collective-permute-start.2 = (bf16[1,512,384]{1,2,0:T(8,128)(2,1)}, bf16[1,512,384]{1,2,0:T(8,128)(2,1)}, u32[]{:S(2)}, u32[]{:S(2)}) collective-permute-start(bf16[1,512,384]{1,2,0:T(8,128)(2,1)} %slice_bitcast_fusion.5), channel_id=1, source_target_pairs={{0,4},{1,5},{2,6},{3,7},{8,12},{9,13},{10,14},{11,15},{16,20},{17,... | collective-permute-start | bytes 1179656 | tf_op jit(solution)/shard_map/ppermute | solution.py:13
  163.8 168.1 %all-gather.17.cloned.1.call-start = ((), (), s32[]{:S(2)}) async-start(), calls=%async_computation.14 | async-start | bytes 7077888 | tf_op jit(solution)/shard_map/all_gather | solution.py:73
  166.0 204.6 %all-gather.21.cloned.1.call-start = ((), (), s32[]{:S(2)}) async-start(), calls=%async_computation.17 | async-start | bytes 1966080 | tf_op jit(solution)/shard_map/all_gather | solution.py:66
  166.8 236.9 %all-gather.19.cloned.1.call-start = ((), (), s32[]{:S(2)}) async-start(), calls=%async_computation.15 | async-start | bytes 3538944 | tf_op jit(solution)/shard_map/all_gather | solution.py:74
  167.5 697.2 %reduce-scatter.14.cloned.1.call-start = ((), (), s32[]{:S(2)}) async-start(), calls=%async_computation.16 | async-start | bytes 1966080 | tf_op jit(solution)/shard_map/reduce_scatter | solution.py:167
  418.5 95.9 %collective-permute-start.3 = (f32[512,1536]{1,0:T(8,128)}, f32[512,1536]{1,0:T(8,128)}, u32[]{:S(2)}, u32[]{:S(2)}) collective-permute-start(f32[512,1536]{1,0:T(8,128)} %convolution_bitcast_fusion.2), channel_id=1, source_target_pairs={{0,1},{1,0},{2,3},{3,2},{4,5},{5,4},{6,7},{7,6},{8,9},{9,8},{10,11... | collective-permute-start | bytes 9437192 | tf_op jit(solution)/shard_map/ppermute | solution.py:188
  423.0 443.5 %reduce-scatter.26.cloned.1.call-start = ((), (), s32[]{:S(2)}) async-start(), calls=%async_computation.23 | async-start | bytes 3538944 | tf_op jit(solution)/shard_map/reduce_scatter | solution.py:304
  519.5 138.1 %collective-permute-start.4 = (f32[512,1536]{1,0:T(8,128)}, f32[512,1536]{1,0:T(8,128)}, u32[]{:S(2)}, u32[]{:S(2)}) collective-permute-start(f32[512,1536]{1,0:T(8,128)} %add.262), channel_id=1, source_target_pairs={{0,2},{1,3},{2,0},{3,1},{4,6},{5,7},{6,4},{7,5},{8,10},{9,11},{10,... | collective-permute-start | bytes 9437192 | tf_op jit(solution)/shard_map/ppermute | solution.py:188
  532.9 335.9 %reduce-scatter.30.cloned.1.call-start = ((), (), s32[]{:S(2)}) async-start(), calls=%async_computation.25 | async-start | bytes 442368
  773.1 51.8 %collective-permute-start.6 = (bf16[1,512,384]{1,2,0:T(8,128)(2,1)}, bf16[1,512,384]{1,2,0:T(8,128)(2,1)}, u32[]{:S(2)}, u32[]{:S(2)}) collective-permute-start(bf16[1,512,384]{1,2,0:T(8,128)(2,1)} %bitcast.100), channel_id=1, source_target_pairs={{4,0},{5,1},{6,2},{7,3},{12,8},{13,9},{14,10},{15,11},{20,16},{21,... | collective-permute-start | bytes 1179656 | tf_op jit(solution)/shard_map/ppermute | solution.py:13
  776.3 44.0 %collective-permute-start.5 = (bf16[1,512,384]{1,2,0:T(8,128)(2,1)}, bf16[1,512,384]{1,2,0:T(8,128)(2,1)}, u32[]{:S(2)}, u32[]{:S(2)}) collective-permute-start(bf16[1,512,384]{1,2,0:T(8,128)(2,1)} %bitcast.90), channel_id=1, source_target_pairs={{4,0},{5,1},{6,2},{7,3},{12,8},{13,9},{14,10},{15,11},{20,16},{21,... | collective-permute-start | bytes 1179656 | tf_op jit(solution)/shard_map/ppermute | solution.py:13
  785.4 6.0 collective-permute-start.7
  819.9 91.7 %reduce-scatter.28.cloned.1.call-start = ((), (), s32[]{:S(2)}) async-start(), calls=%async_computation.24 | async-start | bytes 163840
  835.3 81.7 %reduce-scatter.20.cloned.1.call-start = ((), (), s32[]{:S(2)}) async-start(), calls=%async_computation.20 | async-start | bytes 1327104 | tf_op jit(solution)/shard_map/reduce_scatter | solution.py:295
  839.0 118.1 %reduce-scatter.22.cloned.1.call-start = ((), (), s32[]{:S(2)}) async-start(), calls=%async_computation.21 | async-start | bytes 1327104 | tf_op jit(solution)/shard_map/reduce_scatter | solution.py:298
  843.1 179.1 %reduce-scatter.24.cloned.1.call-start = ((), (), s32[]{:S(2)}) async-start(), calls=%async_computation.22 | async-start | bytes 7077888 | tf_op jit(solution)/shard_map/reduce_scatter | solution.py:301
  857.7 202.1 %reduce-scatter.16.cloned.1.call-start = ((), (), s32[]{:S(2)}) async-start(), calls=%async_computation.18 | async-start | bytes 1966080 | tf_op jit(solution)/shard_map/reduce_scatter | solution.py:273
  858.3 252.3 %reduce-scatter.18.cloned.1.call-start = ((), (), s32[]{:S(2)}) async-start(), calls=%async_computation.19 | async-start | bytes 3981312 | tf_op jit(solution)/shard_map/reduce_scatter | solution.py:289
  (76 other events, 1118.2 us)
Sparse Core Ops, SparseCore 0:
  9.6 39.7 all-gather.8
  51.3 32.8 all-gather.10
  86.1 24.0 all-gather.12
  111.9 24.1 all-gather.14
  163.9 121.0 all-reduce.3
  287.3 44.5 all-gather.16
  333.5 37.0 all-gather.20
  372.5 31.1 all-gather.18
  423.2 58.4 reduce-scatter.13
  533.0 44.3 reduce-scatter.25
  820.1 36.0 reduce-scatter.29
  858.9 19.1 reduce-scatter.27
  881.9 34.9 reduce-scatter.19
  920.4 36.7 reduce-scatter.21
  960.4 61.7 reduce-scatter.23
  1024.4 35.2 reduce-scatter.15
  1063.5 47.0 reduce-scatter.17
